TPU v7x, 32 devices: a whole 2x2x4 slice. The times are simulated.
32 devices in a mesh: row: 2 (over x), col: 4 (over y, core), mode: 4 (over z).
Axes of the slice: x: 2, y: 2, z: 4, core: 2. Of those that a mesh axis runs over, the one named last changes fastest.
Arguments:
- object_field: float32 [2, 512, 1024], P(None, 'row', 'col'), may hold values from -6 to 6
- probe_real: float32 [4, 128, 128], P('mode'), may hold values from -3 to 3
- probe_imag: float32 [4, 128, 128], P('mode'), may hold values from -3 to 3
- amplitude: float32 [2, 4, 8, 128, 128], P('row', 'col'), may hold values from 0 to 3
- positions: int32 [2, 4, 8, 2], P('row', 'col'), may hold values from 0 to 256, as said below
- counts: int32 [2, 4], P('row', 'col'), may hold values from 2 to 8, as said below
Outputs:
- updated: float32 [2, 512, 1024], P(None, 'row', 'col')
Inputs may be any that keep to these rules, and one draw needn't show every extreme that they name: `positions`: offsets lie in 0 to 256 for rows and 0 to 256 for columns. In every tile slot 0 starts within the first 64 rows and columns of the window, and slot 1 ends within the last 64 rows and columns. `counts`: some tile has 8 frames and some tile has 2.
All inputs are finite; a program needn't handle non-finite values.
Results may differ from a plain program's by a relative error of at most 0.0003.
Values sent between devices are 32-bit elements; how exact they have to be, the bound alone decides.
A program may use at most 64 MiB of HBM per device.

v0:
```python
from functools import partial
import jax
import jax.numpy as jnp
from jax import lax
from jax.sharding import PartitionSpec as P

FRAME = 128
MARGIN = 64
SLOTS = 8
STEP_SIZE = 0.25


def padded(cells, sides, width):
    for axis, dim in sides:
        count = lax.axis_size(axis)
        ends = count - 1
        head = lax.slice_in_dim(cells, 0, width, axis=dim)
        tail = lax.slice_in_dim(cells, cells.shape[dim] - width, cells.shape[dim], axis=dim)
        cells = jnp.concatenate(
            [
                lax.ppermute(tail, axis, [(i, (i + 1) % count) for i in range(ends)]),
                cells,
                lax.ppermute(head, axis, [((i + 1) % count, i) for i in range(ends)]),
            ],
            axis=dim,
        )
    return cells


def tables(length):
    counter = jnp.arange(length, dtype=jnp.int32)
    phase = counter[:, None] * counter[None, :] % length
    angles = phase.astype(jnp.float32) * (2.0 * jnp.pi / length)
    factor = 1.0 / jnp.sqrt(jnp.float32(length))
    return (jnp.cos(angles) * factor, jnp.sin(angles) * factor)


def transform(real_part, imag_part, cosine, sine_table, direction):
    product = partial(jnp.matmul, precision=lax.Precision.HIGHEST)
    left_real = product(cosine, real_part) + direction * product(sine_table, imag_part)
    left_imag = product(cosine, imag_part) - direction * product(sine_table, real_part)
    out_real = product(left_real, cosine) + direction * product(left_imag, sine_table)
    out_imag = product(left_imag, cosine) - direction * product(left_real, sine_table)
    return (out_real, out_imag)


def forward_wave(window, mode_real, mode_imag, cosine, sine_table):
    object_real = window[..., 0, :, :]
    object_imag = window[..., 1, :, :]
    wave_real = mode_real * object_real - mode_imag * object_imag
    wave_imag = mode_real * object_imag + mode_imag * object_real
    return transform(wave_real, wave_imag, cosine, sine_table, 1.0)


def backward_wave(
    spec_real, spec_imag, intensity, target, mode_real, mode_imag, cosine, sine_table
):
    keep = 1.0 - target / jnp.maximum(jnp.sqrt(intensity), 1.0)
    back_real, back_imag = transform(spec_real * keep, spec_imag * keep, cosine, sine_table, -1.0)
    grad_real = mode_real * back_real + mode_imag * back_imag
    grad_imag = mode_real * back_imag - mode_imag * back_real
    return jnp.stack([grad_real, grad_imag], axis=-3)


def fold_rims(gradient):
    margin = MARGIN
    borders = jnp.concatenate([gradient[:, :margin], gradient[:, -margin:]], axis=1)
    received = padded(borders, (("row", 1),), margin)
    interior = gradient[:, margin:-margin]
    interior = interior.at[:, :margin].add(received[:, :margin])
    interior = interior.at[:, -margin:].add(received[:, -margin:])
    sideways = jnp.concatenate([interior[:, :, :margin], interior[:, :, -margin:]], axis=2)
    arrived = padded(sideways, (("col", 2),), margin)
    centre = interior[:, :, margin:-margin]
    centre = centre.at[:, :, :margin].add(arrived[:, :, :margin])
    centre = centre.at[:, :, -margin:].add(arrived[:, :, -margin:])
    return centre


def per_device(object_field, probe_real, probe_imag, amplitude, positions, counts):
    cosine, sine_table = tables(FRAME)
    extended = padded(object_field, (("row", 1), ("col", 2)), MARGIN)
    measured = amplitude[0, 0]
    offsets = positions[0, 0]
    active = counts[0, 0]
    anchor = jnp.zeros((), jnp.int32)

    def window_of(slot):
        return lax.dynamic_slice(
            extended, (anchor, offsets[slot, 0], offsets[slot, 1]), (2, FRAME, FRAME)
        )

    def deposit(gradient, slot, contrib):
        weight = (slot < active).astype(jnp.float32)
        corner = (anchor, offsets[slot, 0], offsets[slot, 1])
        previous = lax.dynamic_slice(gradient, corner, (2, FRAME, FRAME))
        return lax.dynamic_update_slice(gradient, previous + contrib * weight, corner)

    gradient = jnp.zeros(extended.shape, jnp.float32)
    all_real, all_imag = (
        lax.all_gather(probe_real, "mode", axis=0, tiled=True),
        lax.all_gather(probe_imag, "mode", axis=0, tiled=True),
    )
    member = lax.axis_index("mode")
    group = lax.axis_size("mode")

    def advance_own(turn, gradient):
        slot = member + turn * group
        spec_real, spec_imag = forward_wave(window_of(slot), all_real, all_imag, cosine, sine_table)
        intensity = jnp.sum(spec_real * spec_real + spec_imag * spec_imag, axis=0)
        terms = backward_wave(
            spec_real, spec_imag, intensity, measured[slot], all_real, all_imag, cosine, sine_table
        )
        return deposit(gradient, slot, jnp.sum(terms, axis=0))

    gradient = lax.fori_loop(0, SLOTS // group, advance_own, gradient)
    summed = lax.psum(gradient, "mode")
    total = fold_rims(summed)
    return object_field - STEP_SIZE * total


def solution(mesh):
    in_specs = (
        P(None, "row", "col"),
        P("mode", None, None),
        P("mode", None, None),
        P("row", "col", None, None, None),
        P("row", "col", None, None),
        P("row", "col"),
    )
    out_specs = P(None, "row", "col")
    return jax.shard_map(
        per_device, mesh=mesh, in_specs=in_specs, out_specs=out_specs, check_vma=False
    )
```

profile of v0, /device:TPU:1, one launch (start us, length us, event | category | flops | bytes accessed | tf_op | source)
XLA Modules:
  0.0 185.5 jit_solution(7516222423846577421)
XLA Ops:
  6.5 1.0 fusion.137
  7.5 3.9 %collective-permute-start = (f32[2,64,256]{2,1,0:T(8,128)S(1)}, f32[2,64,256]{2,1,0:T(8,128)S(1)}, u32[]{:S(2)}, u32[]{:S(2)}) collective-permute-start(f32[2,64,256]{2,1,0:T(8,128)S(1)} %get-tuple-element.375), channel_id=1, source_target_pairs={{0,16},{1,17},{2,18},{3,19},{4,20},{5,21},{6,22},{7,23},{8,24},{9,... | collective-permute-start | bytes 393224 | tf_op jit(solution)/shard_map/ppermute | solution.py:21
  11.5 1.3 collective-permute-start.1
  12.8 0.9 collective-permute-done
  13.6 1.1 constant_dynamic-update-slice_fusion.1
  14.8 2.4 %collective-permute-done.1 = f32[2,64,256]{2,1,0:T(8,128)S(1)} collective-permute-done((f32[2,64,256]{2,1,0:T(8,128)S(1)}, f32[2,64,256]{2,1,0:T(8,128)S(1)}, u32[]{:S(2)}, u32[]{:S(2)}) %collective-permute-start.1) | collective-permute-done | bytes 131104 | tf_op jit(solution)/shard_map/ppermute | solution.py:23
  17.4 5.1 %collective-permute-start.2 = (f32[2,384,64]{2,1,0:T(8,128)S(1)}, f32[2,384,64]{2,1,0:T(8,128)S(1)}, u32[]{:S(2)}, u32[]{:S(2)}) collective-permute-start(f32[2,384,64]{2,1,0:T(8,128)S(1)} %get-tuple-element.372), channel_id=1, source_target_pairs={{0,4},{4,8},{8,12},{1,5},{5,9},{9,13},{2,6},{6,10},{10,14},{3,7},{... | collective-permute-start | bytes 589832 | tf_op jit(solution)/shard_map/ppermute | solution.py:21
  22.5 1.9 %collective-permute-start.3 = (f32[2,384,64]{2,1,0:T(8,128)S(1)}, f32[2,384,64]{2,1,0:T(8,128)S(1)}, u32[]{:S(2)}, u32[]{:S(2)}) collective-permute-start(f32[2,384,64]{2,1,0:T(8,128)S(1)} %get-tuple-element.373), channel_id=1, source_target_pairs={{4,0},{8,4},{12,8},{5,1},{9,5},{13,9},{6,2},{10,6},{14,10},{7,3},{... | collective-permute-start | bytes 589832 | tf_op jit(solution)/shard_map/ppermute | solution.py:23
  24.5 12.1 %all_gather.6 = f32[4,128,128]{2,1,0:T(8,128)S(1)} all-gather(f32[1,128,128]{2,1,0:T(8,128)S(1)} %copy-done.3), channel_id=1, replica_groups=mesh['row'=2,'col'=4,'mode'=4] {'mode'}, dimensions={0}, use_global_device_ids=true | all-gather | bytes 327680 | tf_op jit(solution)/shard_map/all_gather | solution.py:101
  36.5 12.3 %all_gather.7 = f32[4,128,128]{2,1,0:T(8,128)S(1)} all-gather(f32[1,128,128]{2,1,0:T(8,128)S(1)} %copy-done.4), channel_id=1, replica_groups=mesh['row'=2,'col'=4,'mode'=4] {'mode'}, dimensions={0}, use_global_device_ids=true | all-gather | bytes 327680 | tf_op jit(solution)/shard_map/all_gather | solution.py:102
  50.0 40.9 %while.19 = (s32[]{:T(128)}, f32[2,384,384]{2,1,0:T(8,128)S(1)}, s32[]{:T(128)}, s32[8,2]{0,1:T(2,128)S(1)}, f32[2,384,384]{2,1,0:T(8,128)S(1)}, /*index=5*/f32[...) while((s32[]{:T(128)}, f32[2,384,384]{2,1,0:T(8,128)S(1)}, ...), condition=%wide.region_3.4_spmd.clone.clone, body=%wide.region_0.3_spmd.clone.clone.sunk | while | flops 1617362944 | bytes 15466841 | solution.py:116
  54.9 0.8 fusion.219
  55.7 0.8 fusion.220
  57.2 0.8 fusion.216
  58.0 0.8 fusion.217
  60.2 0.7 add_reduce_fusion.2
  60.9 0.9 fusion.222
  62.5 0.7 fusion.227
  63.3 0.7 fusion.223
  64.0 0.7 fusion.224
  67.0 0.7 add_bitcast_fusion.2
  67.9 2.5 %dynamic_update_slice.10 = f32[2,384,384]{2,1,0:T(8,128)S(1)} dynamic-update-slice(f32[2,384,384]{2,1,0:T(8,128)S(1)} %get-tuple-element.463, f32[2,128,128]{2,1,0:T(8,128)S(1)} %multiply_add_fusion.9, s32[]{:T(128)} %constant.176.clone.1..sunk, s32[]{:T(128)S(6)} %select_n.178, s32[]{:T(128)S(6)} %select_n.179) | dynamic-update-slice | bytes 262148 | tf_op jit(solution)/shard_map/while/body/eval_jaxpr/dynamic_update_slice | solution.py:97
  75.3 0.8 fusion.219
  76.1 0.8 fusion.220
  77.6 0.8 fusion.216
  78.4 0.8 fusion.217
  80.6 0.7 add_reduce_fusion.2
  81.4 0.9 fusion.222
  82.2 0.7 fusion.226
  83.0 0.7 fusion.227
  83.7 0.7 fusion.223
  84.5 0.7 fusion.224
  87.4 0.7 add_bitcast_fusion.2
  88.3 2.5 %dynamic_update_slice.10 = f32[2,384,384]{2,1,0:T(8,128)S(1)} dynamic-update-slice(f32[2,384,384]{2,1,0:T(8,128)S(1)} %get-tuple-element.463, f32[2,128,128]{2,1,0:T(8,128)S(1)} %multiply_add_fusion.9, s32[]{:T(128)} %constant.176.clone.1..sunk, s32[]{:T(128)S(6)} %select_n.178, s32[]{:T(128)S(6)} %select_n.179) | dynamic-update-slice | bytes 262148 | tf_op jit(solution)/shard_map/while/body/eval_jaxpr/dynamic_update_slice | solution.py:97
  90.9 1.0 copy-done
  91.9 59.9 %all-reduce.2.cloned.1.call-done = f32[2,384,384]{2,1,0:T(8,128)} async-done(((f32[2,384,384]{2,1,0:T(8,128)}), f32[2,384,384]{2,1,0:T(8,128)}) %all-reduce.2.cloned.1.call-update) | async-done | bytes 1179664 | tf_op jit(solution)/shard_map/psum | solution.py:117
  151.8 1.2 fusion.134
  153.0 3.1 %collective-permute-start.4 = (f32[2,64,384]{2,1,0:T(8,128)S(1)}, f32[2,64,384]{2,1,0:T(8,128)S(1)}, u32[]{:S(2)}, u32[]{:S(2)}) collective-permute-start(f32[2,64,384]{2,1,0:T(8,128)S(1)} %get-tuple-element.369), channel_id=1, source_target_pairs={{0,16},{1,17},{2,18},{3,19},{4,20},{5,21},{6,22},{7,23},{8,24},{9,... | collective-permute-start | bytes 589832 | tf_op jit(solution)/shard_map/ppermute | solution.py:21
  156.1 1.3 collective-permute-start.5
  157.4 2.4 %collective-permute-done.4 = f32[2,64,384]{2,1,0:T(8,128)S(1)} collective-permute-done((f32[2,64,384]{2,1,0:T(8,128)S(1)}, f32[2,64,384]{2,1,0:T(8,128)S(1)}, u32[]{:S(2)}, u32[]{:S(2)}) %collective-permute-start.4) | collective-permute-done | bytes 196640 | tf_op jit(solution)/shard_map/ppermute | solution.py:21
  159.8 3.8 %collective-permute-done.5 = f32[2,64,384]{2,1,0:T(8,128)S(1)} collective-permute-done((f32[2,64,384]{2,1,0:T(8,128)S(1)}, f32[2,64,384]{2,1,0:T(8,128)S(1)}, u32[]{:S(2)}, u32[]{:S(2)}) %collective-permute-start.5) | collective-permute-done | bytes 196640 | tf_op jit(solution)/shard_map/ppermute | solution.py:23
  163.8 4.7 %collective-permute-start.6 = (f32[2,256,64]{2,1,0:T(8,128)S(1)}, f32[2,256,64]{2,1,0:T(8,128)S(1)}, u32[]{:S(2)}, u32[]{:S(2)}) collective-permute-start(f32[2,256,64]{2,1,0:T(8,128)S(1)} %get-tuple-element.371), channel_id=1, source_target_pairs={{0,4},{4,8},{8,12},{1,5},{5,9},{9,13},{2,6},{6,10},{10,14},{3,7},{... | collective-permute-start | bytes 393224 | tf_op jit(solution)/shard_map/ppermute | solution.py:21
  168.7 2.1 %collective-permute-start.7 = (f32[2,256,64]{2,1,0:T(8,128)S(1)}, f32[2,256,64]{2,1,0:T(8,128)S(1)}, u32[]{:S(2)}, u32[]{:S(2)}) collective-permute-start(f32[2,256,64]{2,1,0:T(8,128)S(1)} %get-tuple-element.370), channel_id=1, source_target_pairs={{4,0},{8,4},{12,8},{5,1},{9,5},{13,9},{6,2},{10,6},{14,10},{7,3},{... | collective-permute-start | bytes 393224 | tf_op jit(solution)/shard_map/ppermute | solution.py:23
  170.7 1.0 collective-permute-done.6
  171.9 1.1 scatter-add.16
  173.0 3.5 %collective-permute-done.7 = f32[2,256,64]{2,1,0:T(8,128)S(1)} collective-permute-done((f32[2,256,64]{2,1,0:T(8,128)S(1)}, f32[2,256,64]{2,1,0:T(8,128)S(1)}, u32[]{:S(2)}, u32[]{:S(2)}) %collective-permute-start.7) | collective-permute-done | bytes 131104 | tf_op jit(solution)/shard_map/ppermute | solution.py:23
  176.6 1.2 scatter-add.19
  177.8 0.9 multiply_subtract_fusion.3
  (49 shorter events, 13.2 us)
Async XLA Ops:
  6.5 145.2 %all-reduce.2.cloned.1.call-start = ((), (), s32[]{:S(2)}) async-start(), calls=%async_computation | async-start | bytes 2359296 | tf_op jit(solution)/shard_map/psum | solution.py:117
  7.5 6.1 %collective-permute-start = (f32[2,64,256]{2,1,0:T(8,128)S(1)}, f32[2,64,256]{2,1,0:T(8,128)S(1)}, u32[]{:S(2)}, u32[]{:S(2)}) collective-permute-start(f32[2,64,256]{2,1,0:T(8,128)S(1)} %get-tuple-element.375), channel_id=1, source_target_pairs={{0,16},{1,17},{2,18},{3,19},{4,20},{5,21},{6,22},{7,23},{8,24},{9,... | collective-permute-start | bytes 393224 | tf_op jit(solution)/shard_map/ppermute | solution.py:21
  11.5 5.7 %collective-permute-start.1 = (f32[2,64,256]{2,1,0:T(8,128)S(1)}, f32[2,64,256]{2,1,0:T(8,128)S(1)}, u32[]{:S(2)}, u32[]{:S(2)}) collective-permute-start(f32[2,64,256]{2,1,0:T(8,128)S(1)} %get-tuple-element.374), channel_id=1, source_target_pairs={{16,0},{17,1},{18,2},{19,3},{20,4},{21,5},{22,6},{23,7},{24,8},{25... | collective-permute-start | bytes 393224 | tf_op jit(solution)/shard_map/ppermute | solution.py:23
  14.7 9.7 %copy-start.3 = (f32[1,128,128]{2,1,0:T(8,128)S(1)}, f32[1,128,128]{2,1,0:T(8,128)}, u32[]{:S(2)}) copy-start(f32[1,128,128]{2,1,0:T(8,128)} %param.17) | copy-start | bytes 196612
  14.7 21.8 %copy-start.4 = (f32[1,128,128]{2,1,0:T(8,128)S(1)}, f32[1,128,128]{2,1,0:T(8,128)}, u32[]{:S(2)}) copy-start(f32[1,128,128]{2,1,0:T(8,128)} %param.18) | copy-start | bytes 196612
  17.4 31.4 %collective-permute-start.2 = (f32[2,384,64]{2,1,0:T(8,128)S(1)}, f32[2,384,64]{2,1,0:T(8,128)S(1)}, u32[]{:S(2)}, u32[]{:S(2)}) collective-permute-start(f32[2,384,64]{2,1,0:T(8,128)S(1)} %get-tuple-element.372), channel_id=1, source_target_pairs={{0,4},{4,8},{8,12},{1,5},{5,9},{9,13},{2,6},{6,10},{10,14},{3,7},{... | collective-permute-start | bytes 589832 | tf_op jit(solution)/shard_map/ppermute | solution.py:21
  22.5 26.3 %collective-permute-start.3 = (f32[2,384,64]{2,1,0:T(8,128)S(1)}, f32[2,384,64]{2,1,0:T(8,128)S(1)}, u32[]{:S(2)}, u32[]{:S(2)}) collective-permute-start(f32[2,384,64]{2,1,0:T(8,128)S(1)} %get-tuple-element.373), channel_id=1, source_target_pairs={{4,0},{8,4},{12,8},{5,1},{9,5},{13,9},{6,2},{10,6},{14,10},{7,3},{... | collective-permute-start | bytes 589832 | tf_op jit(solution)/shard_map/ppermute | solution.py:23
  49.3 0.7 copy-start.5
  90.9 1.0 copy-start
  151.8 8.0 %copy-start.1 = (f32[2,384,384]{2,1,0:T(8,128)S(1)}, f32[2,384,384]{2,1,0:T(8,128)}, u32[]{:S(2)}) copy-start(f32[2,384,384]{2,1,0:T(8,128)} %all-reduce.2.cloned.1.call-done) | copy-start | bytes 3538948
  151.8 8.0 %slice-start = ((f32[2,384,384]{2,1,0:T(8,128)}), f32[2,256,384]{2,1,0:T(8,128)S(1)}, s32[]{:S(2)}) async-start(f32[2,384,384]{2,1,0:T(8,128)} %all-reduce.2.cloned.1.call-done), calls=%async_computation.1 | async-start | bytes 1572864 | tf_op jit(solution)/shard_map/slice | solution.py:69
  153.0 6.8 %collective-permute-start.4 = (f32[2,64,384]{2,1,0:T(8,128)S(1)}, f32[2,64,384]{2,1,0:T(8,128)S(1)}, u32[]{:S(2)}, u32[]{:S(2)}) collective-permute-start(f32[2,64,384]{2,1,0:T(8,128)S(1)} %get-tuple-element.369), channel_id=1, source_target_pairs={{0,16},{1,17},{2,18},{3,19},{4,20},{5,21},{6,22},{7,23},{8,24},{9,... | collective-permute-start | bytes 589832 | tf_op jit(solution)/shard_map/ppermute | solution.py:21
  156.1 7.5 %collective-permute-start.5 = (f32[2,64,384]{2,1,0:T(8,128)S(1)}, f32[2,64,384]{2,1,0:T(8,128)S(1)}, u32[]{:S(2)}, u32[]{:S(2)}) collective-permute-start(f32[2,64,384]{2,1,0:T(8,128)S(1)} %get-tuple-element.368), channel_id=1, source_target_pairs={{16,0},{17,1},{18,2},{19,3},{20,4},{21,5},{22,6},{23,7},{24,8},{25... | collective-permute-start | bytes 589832 | tf_op jit(solution)/shard_map/ppermute | solution.py:23
  163.8 8.0 %collective-permute-start.6 = (f32[2,256,64]{2,1,0:T(8,128)S(1)}, f32[2,256,64]{2,1,0:T(8,128)S(1)}, u32[]{:S(2)}, u32[]{:S(2)}) collective-permute-start(f32[2,256,64]{2,1,0:T(8,128)S(1)} %get-tuple-element.371), channel_id=1, source_target_pairs={{0,4},{4,8},{8,12},{1,5},{5,9},{9,13},{2,6},{6,10},{10,14},{3,7},{... | collective-permute-start | bytes 393224 | tf_op jit(solution)/shard_map/ppermute | solution.py:21
  168.7 9.2 %copy-start.2 = (f32[2,256,256]{2,1,0:T(8,128)S(1)}, f32[2,256,256]{2,1,0:T(8,128)}, u32[]{:S(2)}) copy-start(f32[2,256,256]{2,1,0:T(8,128)} %param.16) | copy-start | bytes 1572868
  168.7 7.8 %collective-permute-start.7 = (f32[2,256,64]{2,1,0:T(8,128)S(1)}, f32[2,256,64]{2,1,0:T(8,128)S(1)}, u32[]{:S(2)}, u32[]{:S(2)}) collective-permute-start(f32[2,256,64]{2,1,0:T(8,128)S(1)} %get-tuple-element.370), channel_id=1, source_target_pairs={{4,0},{8,4},{12,8},{5,1},{9,5},{13,9},{6,2},{10,6},{14,10},{7,3},{... | collective-permute-start | bytes 393224 | tf_op jit(solution)/shard_map/ppermute | solution.py:23
Sparse Core Ops, SparseCore 0:
  92.0 59.7 all-reduce.1
where the time goes:
time: 186 us
  waiting for transfers between devices  73.9 us (40%)
  blocking collectives  24.4 us (13%)
  matrix products  23.7 us (13%)
  starting transfers between devices  23.4 us (13%)
  local copies, waits for them, and re-layouts  14.2 us (8%)
  between operations  13.6 us (7%)
  loops' own time  8.74 us (5%)
  other arithmetic  3.71 us (2%)
    psum x1, waiting for transfers between devices, per_device(): summed = lax.psum(gradient, 'mode')  59.9 us
    ppermute x4, starting transfers between devices, padded(): lax.ppermute(tail, axis, [(i, (i + 1) % count) for i in range(ends)])  16.9 us
    all_gather x1, blocking collectives, per_device(): lax.all_gather(probe_imag, 'mode', axis=0, tiled=True)  12.3 us
    all_gather x1, blocking collectives, per_device(): lax.all_gather(probe_real, 'mode', axis=0, tiled=True)  12.1 us
    ppermute x4, waiting for transfers between devices, padded(): lax.ppermute(head, axis, [((i + 1) % count, i) for i in range(ends)])  9.72 us
    another operation x1, loops' own time, per_device(): gradient = lax.fori_loop(0, SLOTS // group, advance_own, gradient)  8.74 us
    ppermute x4, starting transfers between devices, padded(): lax.ppermute(head, axis, [((i + 1) % count, i) for i in range(ends)])  6.56 us
    dynamic_update_slice x2, local copies, waits for them, and re-layouts, deposit(): lax.dynamic_update_slice(gradient, previous + contrib * weight, corner)  4.99 us
  transfers between devices with their start and end apart: 9, of which 7 were waited for; matrix products, arithmetic and copies ran while one was open for 1% of the time, Pallas kernels for 0%

commit v1 on v0

--- a/solution.py
+++ b/solution.py
@@ -114,7 +114,8 @@
         return deposit(gradient, slot, jnp.sum(terms, axis=0))
 
     gradient = lax.fori_loop(0, SLOTS // group, advance_own, gradient)
-    summed = lax.psum(gradient, "mode")
+    stacks_all_view = lambda field_in: jax.lax.all_gather(field_in, axis_name="mode").sum(axis=0)
+    summed = stacks_all_view(gradient)
     total = fold_rims(summed)
     return object_field - STEP_SIZE * total
 

time: 186 us -> 222 us (1.19)
  waiting for transfers between devices: 73.9 us -> 107 us
  other arithmetic: 3.71 us -> 6.43 us
    all_gather x0 -> x1, waiting for transfers between devices: none -> 93.1 us  [per_device(): jax.lax.all_gather(field_in, axis_name='mode').sum(axis=0)]
    psum x1 -> x0, waiting for transfers between devices: 59.9 us -> none  [per_device(): summed = lax.psum(gradient, 'mode')]
    reduce_sum x0 -> x1, other arithmetic: none -> 2.72 us  [per_device(): jax.lax.all_gather(field_in, axis_name='mode').sum(axis=0)]
where the time goes in v1:
time: 222 us; the launch traced here: 221 us
  waiting for transfers between devices  107 us (48%)
  blocking collectives  24.4 us (11%)
  matrix products  23.7 us (11%)
  starting transfers between devices  23.6 us (11%)
  between operations  13.6 us (6%)
  local copies, waits for them, and re-layouts  13.2 us (6%)
  loops' own time  9.21 us (4%)
  other arithmetic  6.43 us (3%)
    all_gather x1, waiting for transfers between devices, per_device(): jax.lax.all_gather(field_in, axis_name='mode').sum(axis=0)  93.1 us
    ppermute x4, starting transfers between devices, padded(): lax.ppermute(tail, axis, [(i, (i + 1) % count) for i in range(ends)])  17 us
    all_gather x1, blocking collectives, per_device(): lax.all_gather(probe_imag, 'mode', axis=0, tiled=True)  12.3 us
    all_gather x1, blocking collectives, per_device(): lax.all_gather(probe_real, 'mode', axis=0, tiled=True)  12.1 us
    ppermute x4, waiting for transfers between devices, padded(): lax.ppermute(head, axis, [((i + 1) % count, i) for i in range(ends)])  9.79 us
    another operation x1, loops' own time, per_device(): gradient = lax.fori_loop(0, SLOTS // group, advance_own, gradient)  9.21 us
    ppermute x4, starting transfers between devices, padded(): lax.ppermute(head, axis, [((i + 1) % count, i) for i in range(ends)])  6.56 us
    dynamic_update_slice x2, local copies, waits for them, and re-layouts, deposit(): lax.dynamic_update_slice(gradient, previous + contrib * weight, corner)  4.99 us
  transfers between devices with their start and end apart: 9, of which 7 were waited for; matrix products, arithmetic and copies ran while one was open for 1% of the time, Pallas kernels for 0%

profile of v1, /device:TPU:1, one launch (start us, length us, event | category | flops | bytes accessed | tf_op | source)
XLA Modules:
  0.0 221.0 jit_solution(14610608037648612115)
XLA Ops:
  6.5 1.0 fusion.137
  7.5 3.9 %collective-permute-start = (f32[2,64,256]{2,1,0:T(8,128)S(1)}, f32[2,64,256]{2,1,0:T(8,128)S(1)}, u32[]{:S(2)}, u32[]{:S(2)}) collective-permute-start(f32[2,64,256]{2,1,0:T(8,128)S(1)} %get-tuple-element.375), channel_id=1, source_target_pairs={{0,16},{1,17},{2,18},{3,19},{4,20},{5,21},{6,22},{7,23},{8,24},{9,... | collective-permute-start | bytes 393224 | tf_op jit(solution)/shard_map/ppermute | solution.py:21
  11.5 1.3 collective-permute-start.1
  12.8 0.9 collective-permute-done
  13.6 1.1 constant_dynamic-update-slice_fusion.1
  14.8 2.4 %collective-permute-done.1 = f32[2,64,256]{2,1,0:T(8,128)S(1)} collective-permute-done((f32[2,64,256]{2,1,0:T(8,128)S(1)}, f32[2,64,256]{2,1,0:T(8,128)S(1)}, u32[]{:S(2)}, u32[]{:S(2)}) %collective-permute-start.1) | collective-permute-done | bytes 131104 | tf_op jit(solution)/shard_map/ppermute | solution.py:23
  17.4 5.1 %collective-permute-start.2 = (f32[2,384,64]{2,1,0:T(8,128)S(1)}, f32[2,384,64]{2,1,0:T(8,128)S(1)}, u32[]{:S(2)}, u32[]{:S(2)}) collective-permute-start(f32[2,384,64]{2,1,0:T(8,128)S(1)} %get-tuple-element.372), channel_id=1, source_target_pairs={{0,4},{4,8},{8,12},{1,5},{5,9},{9,13},{2,6},{6,10},{10,14},{3,7},{... | collective-permute-start | bytes 589832 | tf_op jit(solution)/shard_map/ppermute | solution.py:21
  22.5 1.9 collective-permute-start.3
  24.5 12.1 %all_gather.12 = f32[4,128,128]{2,1,0:T(8,128)S(1)} all-gather(f32[1,128,128]{2,1,0:T(8,128)S(1)} %copy-done.2), channel_id=1, replica_groups=mesh['row'=2,'col'=4,'mode'=4] {'mode'}, dimensions={0}, use_global_device_ids=true | all-gather | bytes 327680 | tf_op jit(solution)/shard_map/all_gather | solution.py:101
  36.5 12.3 %all_gather.13 = f32[4,128,128]{2,1,0:T(8,128)S(1)} all-gather(f32[1,128,128]{2,1,0:T(8,128)S(1)} %copy-done.3), channel_id=1, replica_groups=mesh['row'=2,'col'=4,'mode'=4] {'mode'}, dimensions={0}, use_global_device_ids=true | all-gather | bytes 327680 | tf_op jit(solution)/shard_map/all_gather | solution.py:102
  50.0 41.5 %while.19 = (s32[]{:T(128)}, f32[2,384,384]{2,1,0:T(8,128)S(1)}, s32[]{:T(128)}, s32[8,2]{0,1:T(2,128)S(1)}, f32[2,384,384]{2,1,0:T(8,128)S(1)}, /*index=5*/f32[...) while((s32[]{:T(128)}, f32[2,384,384]{2,1,0:T(8,128)S(1)}, ...), condition=%wide.region_3.4_spmd.clone.clone, body=%wide.region_0.3_spmd.clone.clone.sunk | while | flops 1617362944 | bytes 15466841 | solution.py:116
  55.1 0.8 fusion.219
  55.9 0.8 fusion.220
  57.4 0.8 fusion.216
  58.2 0.8 fusion.217
  60.4 0.7 add_reduce_fusion.2
  61.1 0.9 fusion.222
  62.0 0.7 fusion.226
  62.8 0.7 fusion.227
  63.5 0.7 fusion.223
  64.3 0.7 fusion.224
  67.2 0.7 add_bitcast_fusion.2
  68.1 2.5 %dynamic_update_slice.10 = f32[2,384,384]{2,1,0:T(8,128)S(1)} dynamic-update-slice(f32[2,384,384]{2,1,0:T(8,128)S(1)} %get-tuple-element.463, f32[2,128,128]{2,1,0:T(8,128)S(1)} %multiply_add_fusion.9, s32[]{:T(128)} %constant.177.clone.1..sunk, s32[]{:T(128)S(6)} %select_n.178, s32[]{:T(128)S(6)} %select_n.179) | dynamic-update-slice | bytes 262148 | tf_op jit(solution)/shard_map/while/body/eval_jaxpr/dynamic_update_slice | solution.py:97
  75.8 0.8 fusion.219
  76.6 0.8 fusion.220
  78.0 0.8 fusion.216
  78.8 0.8 fusion.217
  81.0 0.7 add_reduce_fusion.2
  81.8 0.9 fusion.222
  83.4 0.7 fusion.227
  84.2 0.7 fusion.223
  84.9 0.7 fusion.224
  87.8 0.7 add_bitcast_fusion.2
  88.8 2.5 %dynamic_update_slice.10 = f32[2,384,384]{2,1,0:T(8,128)S(1)} dynamic-update-slice(f32[2,384,384]{2,1,0:T(8,128)S(1)} %get-tuple-element.463, f32[2,128,128]{2,1,0:T(8,128)S(1)} %multiply_add_fusion.9, s32[]{:T(128)} %constant.177.clone.1..sunk, s32[]{:T(128)S(6)} %select_n.178, s32[]{:T(128)S(6)} %select_n.179) | dynamic-update-slice | bytes 262148 | tf_op jit(solution)/shard_map/while/body/eval_jaxpr/dynamic_update_slice | solution.py:97
  91.5 1.0 copy-done
  92.5 93.1 %all-gather.3.cloned.1.call-done = f32[8,384,384]{2,1,0:T(8,128)} async-done(((f32[2,384,384]{2,1,0:T(8,128)}), f32[8,384,384]{2,1,0:T(8,128)}) %all-gather.3.cloned.1.call-update) | async-done | bytes 4718608 | tf_op jit(solution)/shard_map/all_gather | solution.py:117
  185.7 2.7 %reduce_sum.35 = f32[2,384,384]{2,1,0:T(8,128)S(1)} reduce(f32[4,2,384,384]{3,2,1,0:T(8,128)} %bitcast.144, f32[]{:T(128)} %constant.178.clone.1), dimensions={0}, to_apply=%region_4.5 | reduce | flops 884736 | bytes 5898244 | tf_op jit(solution)/shard_map/reduce_sum | solution.py:117
  188.4 3.1 %collective-permute-start.4 = (f32[2,64,384]{2,1,0:T(8,128)S(1)}, f32[2,64,384]{2,1,0:T(8,128)S(1)}, u32[]{:S(2)}, u32[]{:S(2)}) collective-permute-start(f32[2,64,384]{2,1,0:T(8,128)S(1)} %get-tuple-element.369), channel_id=1, source_target_pairs={{0,16},{1,17},{2,18},{3,19},{4,20},{5,21},{6,22},{7,23},{8,24},{9,... | collective-permute-start | bytes 589832 | tf_op jit(solution)/shard_map/ppermute | solution.py:21
  191.6 1.3 collective-permute-start.5
  192.9 2.1 collective-permute-done.4
  195.0 3.9 %collective-permute-done.5 = f32[2,64,384]{2,1,0:T(8,128)S(1)} collective-permute-done((f32[2,64,384]{2,1,0:T(8,128)S(1)}, f32[2,64,384]{2,1,0:T(8,128)S(1)}, u32[]{:S(2)}, u32[]{:S(2)}) %collective-permute-start.5) | collective-permute-done | bytes 196640 | tf_op jit(solution)/shard_map/ppermute | solution.py:23
  199.1 4.9 %collective-permute-start.6 = (f32[2,256,64]{2,1,0:T(8,128)S(1)}, f32[2,256,64]{2,1,0:T(8,128)S(1)}, u32[]{:S(2)}, u32[]{:S(2)}) collective-permute-start(f32[2,256,64]{2,1,0:T(8,128)S(1)} %get-tuple-element.371), channel_id=1, source_target_pairs={{0,4},{4,8},{8,12},{1,5},{5,9},{9,13},{2,6},{6,10},{10,14},{3,7},{... | collective-permute-start | bytes 393224 | tf_op jit(solution)/shard_map/ppermute | solution.py:21
  204.2 2.1 collective-permute-start.7
  206.2 1.0 collective-permute-done.6
  207.4 1.1 scatter-add.16
  208.5 3.5 %collective-permute-done.7 = f32[2,256,64]{2,1,0:T(8,128)S(1)} collective-permute-done((f32[2,256,64]{2,1,0:T(8,128)S(1)}, f32[2,256,64]{2,1,0:T(8,128)S(1)}, u32[]{:S(2)}, u32[]{:S(2)}) %collective-permute-start.7) | collective-permute-done | bytes 131104 | tf_op jit(solution)/shard_map/ppermute | solution.py:23
  212.1 1.2 scatter-add.19
  213.3 0.9 multiply_subtract_fusion.3
  (47 shorter events, 13.4 us)
Async XLA Ops:
  6.5 179.1 %all-gather.3.cloned.1.call-start = ((), (), s32[]{:S(2)}) async-start(), calls=%async_computation | async-start | bytes 5898240 | tf_op jit(solution)/shard_map/all_gather | solution.py:117
  7.5 6.1 %collective-permute-start = (f32[2,64,256]{2,1,0:T(8,128)S(1)}, f32[2,64,256]{2,1,0:T(8,128)S(1)}, u32[]{:S(2)}, u32[]{:S(2)}) collective-permute-start(f32[2,64,256]{2,1,0:T(8,128)S(1)} %get-tuple-element.375), channel_id=1, source_target_pairs={{0,16},{1,17},{2,18},{3,19},{4,20},{5,21},{6,22},{7,23},{8,24},{9,... | collective-permute-start | bytes 393224 | tf_op jit(solution)/shard_map/ppermute | solution.py:21
  11.5 5.7 %collective-permute-start.1 = (f32[2,64,256]{2,1,0:T(8,128)S(1)}, f32[2,64,256]{2,1,0:T(8,128)S(1)}, u32[]{:S(2)}, u32[]{:S(2)}) collective-permute-start(f32[2,64,256]{2,1,0:T(8,128)S(1)} %get-tuple-element.374), channel_id=1, source_target_pairs={{16,0},{17,1},{18,2},{19,3},{20,4},{21,5},{22,6},{23,7},{24,8},{25... | collective-permute-start | bytes 393224 | tf_op jit(solution)/shard_map/ppermute | solution.py:23
  14.7 9.7 %copy-start.2 = (f32[1,128,128]{2,1,0:T(8,128)S(1)}, f32[1,128,128]{2,1,0:T(8,128)}, u32[]{:S(2)}) copy-start(f32[1,128,128]{2,1,0:T(8,128)} %param.17) | copy-start | bytes 196612
  14.7 21.8 %copy-start.3 = (f32[1,128,128]{2,1,0:T(8,128)S(1)}, f32[1,128,128]{2,1,0:T(8,128)}, u32[]{:S(2)}) copy-start(f32[1,128,128]{2,1,0:T(8,128)} %param.18) | copy-start | bytes 196612
  17.4 31.4 %collective-permute-start.2 = (f32[2,384,64]{2,1,0:T(8,128)S(1)}, f32[2,384,64]{2,1,0:T(8,128)S(1)}, u32[]{:S(2)}, u32[]{:S(2)}) collective-permute-start(f32[2,384,64]{2,1,0:T(8,128)S(1)} %get-tuple-element.372), channel_id=1, source_target_pairs={{0,4},{4,8},{8,12},{1,5},{5,9},{9,13},{2,6},{6,10},{10,14},{3,7},{... | collective-permute-start | bytes 589832 | tf_op jit(solution)/shard_map/ppermute | solution.py:21
  22.5 26.3 %collective-permute-start.3 = (f32[2,384,64]{2,1,0:T(8,128)S(1)}, f32[2,384,64]{2,1,0:T(8,128)S(1)}, u32[]{:S(2)}, u32[]{:S(2)}) collective-permute-start(f32[2,384,64]{2,1,0:T(8,128)S(1)} %get-tuple-element.373), channel_id=1, source_target_pairs={{4,0},{8,4},{12,8},{5,1},{9,5},{13,9},{6,2},{10,6},{14,10},{7,3},{... | collective-permute-start | bytes 589832 | tf_op jit(solution)/shard_map/ppermute | solution.py:23
  49.3 0.7 copy-start.4
  91.5 1.0 copy-start
  188.4 6.6 %collective-permute-start.4 = (f32[2,64,384]{2,1,0:T(8,128)S(1)}, f32[2,64,384]{2,1,0:T(8,128)S(1)}, u32[]{:S(2)}, u32[]{:S(2)}) collective-permute-start(f32[2,64,384]{2,1,0:T(8,128)S(1)} %get-tuple-element.369), channel_id=1, source_target_pairs={{0,16},{1,17},{2,18},{3,19},{4,20},{5,21},{6,22},{7,23},{8,24},{9,... | collective-permute-start | bytes 589832 | tf_op jit(solution)/shard_map/ppermute | solution.py:21
  191.6 7.3 %collective-permute-start.5 = (f32[2,64,384]{2,1,0:T(8,128)S(1)}, f32[2,64,384]{2,1,0:T(8,128)S(1)}, u32[]{:S(2)}, u32[]{:S(2)}) collective-permute-start(f32[2,64,384]{2,1,0:T(8,128)S(1)} %get-tuple-element.368), channel_id=1, source_target_pairs={{16,0},{17,1},{18,2},{19,3},{20,4},{21,5},{22,6},{23,7},{24,8},{25... | collective-permute-start | bytes 589832 | tf_op jit(solution)/shard_map/ppermute | solution.py:23
  199.1 8.2 %collective-permute-start.6 = (f32[2,256,64]{2,1,0:T(8,128)S(1)}, f32[2,256,64]{2,1,0:T(8,128)S(1)}, u32[]{:S(2)}, u32[]{:S(2)}) collective-permute-start(f32[2,256,64]{2,1,0:T(8,128)S(1)} %get-tuple-element.371), channel_id=1, source_target_pairs={{0,4},{4,8},{8,12},{1,5},{5,9},{9,13},{2,6},{6,10},{10,14},{3,7},{... | collective-permute-start | bytes 393224 | tf_op jit(solution)/shard_map/ppermute | solution.py:21
  204.2 9.2 %copy-start.1 = (f32[2,256,256]{2,1,0:T(8,128)S(1)}, f32[2,256,256]{2,1,0:T(8,128)}, u32[]{:S(2)}) copy-start(f32[2,256,256]{2,1,0:T(8,128)} %param.16) | copy-start | bytes 1572868
  204.2 7.8 %collective-permute-start.7 = (f32[2,256,64]{2,1,0:T(8,128)S(1)}, f32[2,256,64]{2,1,0:T(8,128)S(1)}, u32[]{:S(2)}, u32[]{:S(2)}) collective-permute-start(f32[2,256,64]{2,1,0:T(8,128)S(1)} %get-tuple-element.370), channel_id=1, source_target_pairs={{4,0},{8,4},{12,8},{5,1},{9,5},{13,9},{6,2},{10,6},{14,10},{7,3},{... | collective-permute-start | bytes 393224 | tf_op jit(solution)/shard_map/ppermute | solution.py:23
Sparse Core Ops, SparseCore 0:
  92.6 92.9 all-gather.2
